TPU v7x, 128 devices: a whole 4x4x4 slice. The times are simulated.
128 devices in a mesh: seq: 32 (over y, z, core), chan: 4 (over x).
Axes of the slice: x: 4, y: 4, z: 4, core: 2. Of those that a mesh axis runs over, the one named last changes fastest.
Arguments:
- tokens: bfloat16 [16384, 4096], P('seq', 'chan'), may hold values from -6 to 6
- in_weight: bfloat16 [4096, 3, 2048], P(None, None, 'chan'), may hold values from -0.09375 to 0.09375
- short_weight: float32 [3, 3, 2048], P(None, None, 'chan'), may hold values from -3 to 3
- filter_taps: float32 [16384, 2048], P('seq', 'chan'), may hold values from -1.1 to 1.1
- skip_gain: float32 [2048], P('chan'), may hold values from -3 to 3
Outputs:
- hyena_out: bfloat16 [16384, 2048], P('seq', 'chan')
All inputs are finite; a program needn't handle non-finite values.
Results may differ from a plain program's by a relative error of at most 0.012.
Values may be sent and summed in bfloat16 or wider, within the bound.
A program may use at most 128 MiB of HBM per device.

v0:
```python
import jax
import jax.numpy as jnp
import numpy as np
from jax import lax
from jax.sharding import PartitionSpec as P

exact = lax.Precision.HIGHEST
SIDE = 128


def transform_tables():
    n = np.arange(SIDE)
    odd = n + 0.5
    first = -2.0 * np.pi / (2 * SIDE) * np.outer(odd, n)
    turn = -2.0 * np.pi / (2 * SIDE * SIDE) * np.outer(odd, n)
    second = -2.0 * np.pi / SIDE * np.outer(n, n)
    wide = np.concatenate([np.cos(first), np.sin(first)], 0)
    cos2, sin2 = (np.cos(second), np.sin(second))
    mix = np.block([[cos2, sin2], [-sin2, cos2]])
    back = np.block([[cos2, -sin2], [sin2, cos2]]) / (SIDE * SIDE)
    return [np.asarray(a, np.float32) for a in (wide, np.cos(turn), np.sin(turn), mix, back)]


def forward(x, tables):
    wide, cosine, sine, mix, _ = tables
    a = jnp.einsum("kn,cnm->ckm", wide, x, precision=exact)
    re, im = (a[:, :SIDE], a[:, SIDE:])
    turned = jnp.concatenate([re * cosine - im * sine, re * sine + im * cosine], axis=2)
    b = jnp.einsum("ckm,mf->ckf", turned, mix, precision=exact)
    return (b[:, :, :SIDE], b[:, :, SIDE:])


def inverse(re, im, tables):
    wide, cosine, sine, _, back = tables
    c = jnp.einsum("ckf,fm->ckm", jnp.concatenate([re, im], axis=2), back, precision=exact)
    re, im = (c[:, :, :SIDE], c[:, :, SIDE:])
    turned = jnp.concatenate([re * cosine + im * sine, im * cosine - re * sine], axis=1)
    return jnp.einsum("kn,ckm->cnm", wide, turned, precision=exact)


def local(tokens, in_weight, short_weight, filter_taps, skip_gain):
    rows, channels = filter_taps.shape
    seq_count = lax.axis_size("seq")
    own = channels // seq_count
    tables = transform_tables()

    def to_channels(values):
        parts = values.astype(jnp.bfloat16).T.reshape(seq_count, own, rows)
        parts = lax.all_to_all(parts, "seq", 0, 0, tiled=True)
        return parts.astype(jnp.float32).transpose(1, 0, 2).reshape(own, SIDE, SIDE)

    filter_re, filter_im = forward(to_channels(filter_taps), tables)
    projected = jnp.einsum(
        "td,dgc->tgc",
        lax.all_gather(tokens, "chan", axis=1, tiled=True),
        in_weight,
        preferred_element_type=jnp.float32,
    ).astype(jnp.bfloat16)
    pairs = [(i, i + 1) for i in range(seq_count - 1)]
    previous = lax.ppermute(projected[rows - 2 :], "seq", pairs)
    extended = jnp.concatenate([previous, projected], axis=0).astype(jnp.float32)
    shorted = (
        short_weight[0] * extended[2:]
        + short_weight[1] * extended[1:-1]
        + short_weight[2] * extended[:-2]
    ).astype(jnp.bfloat16)
    short_f32 = shorted.astype(jnp.float32)
    mixed_in = short_f32[:, 1] * short_f32[:, 2]
    data_re, data_im = forward(to_channels(mixed_in), tables)
    prod_re = data_re * filter_re - data_im * filter_im
    prod_im = data_re * filter_im + data_im * filter_re
    result = inverse(prod_re, prod_im, tables)
    parts = result.reshape(own, seq_count, rows).transpose(1, 0, 2).astype(jnp.bfloat16)
    parts = lax.all_to_all(parts, "seq", 0, 0, tiled=True)
    conv_vals = parts.reshape(channels, rows).T.astype(jnp.float32)
    return ((conv_vals + skip_gain * mixed_in) * short_f32[:, 0]).astype(jnp.bfloat16)


def solution(mesh):
    return jax.shard_map(
        local,
        mesh=mesh,
        in_specs=(
            P("seq", "chan"),
            P(None, None, "chan"),
            P(None, None, "chan"),
            P("seq", "chan"),
            P("chan"),
        ),
        out_specs=P("seq", "chan"),
        check_vma=False,
    )
```

profile of v0, /device:TPU:1, one launch (start us, length us, event | category | flops | bytes accessed | tf_op | source)
XLA Modules:
  0.0 156.6 jit_solution(4305946872558617440)
XLA Ops:
  7.3 2.2 %copy.35 = bf16[512,512]{0,1:T(8,128)(2,1)} copy(f32[512,512]{1,0:T(8,128)} %param.16) | data formatting | bytes 1572864 | tf_op args[3]
  9.5 9.6 %all-to-all-start.1 = ((bf16[32,16,512]{2,1,0:T(8,128)(2,1)}), bf16[32,16,512]{2,1,0:T(8,128)(2,1)}, u32[]{:S(2)}, u32[]{:S(2)}) async-start(bf16[32,16,512]{2,1,0:T(8,128)(2,1)} %bitcast.12), calls=%async_computation.1 | async-start | bytes 1048576 | tf_op jit(solution)/shard_map/all_to_all | solution.py:49
  19.2 41.1 %all-gather.2.cloned.1.call-done = bf16[512,4096]{1,0:T(8,128)(2,1)} async-done(((bf16[512,1024]{1,0:T(8,128)(2,1)}), bf16[512,4096]{1,0:T(8,128)(2,1)}) %all-gather.2.cloned.1.call-update) | async-done | bytes 4194320 | tf_op jit(solution)/shard_map/all_gather | solution.py:55
  60.2 10.9 %fusion.21 = bf16[512,3,512]{2,0,1:T(8,128)(2,1)S(1)} fusion(bf16[4096,3,512]{2,0,1:T(8,128)(2,1)} %param.14, bf16[512,4096]{1,0:T(8,128)(2,1)} %all-gather.2.cloned.1.call-done), kind=kOutput, calls=%fused_computation.24 | convolution fusion | flops 6443237376 | bytes 18350080 | tf_op jit(solution)/shard_map/td,dgc->tgc/dot_general | solution.py:53
  71.1 3.9 %collective-permute-start = (bf16[2,3,512]{2,0,1:T(2,128)(2,1)S(1)}, bf16[2,3,512]{2,0,1:T(2,128)(2,1)S(1)}, u32[]{:S(2)}, u32[]{:S(2)}) collective-permute-start(bf16[2,3,512]{2,0,1:T(2,128)(2,1)S(1)} %slice.80), channel_id=1, source_target_pairs={{0,4},{4,8},{8,12},{12,16},{16,20},{20,24},{24,28},{28,32},{32,36}... | collective-permute-start | bytes 18440 | tf_op jit(solution)/shard_map/ppermute | solution.py:60
  78.2 2.0 %copy.31 = bf16[512,512]{1,0:T(8,128)(2,1)} copy(bf16[512,512]{0,1:T(8,128)(2,1)} %convert_bitcast_fusion) | data formatting | bytes 1048576 | tf_op jit(solution)/shard_map/transpose | solution.py:48
  80.2 8.5 %all-to-all-start = ((bf16[32,16,512]{2,1,0:T(8,128)(2,1)}), bf16[32,16,512]{2,1,0:T(8,128)(2,1)}, u32[]{:S(2)}, u32[]{:S(2)}) async-start(bf16[32,16,512]{2,1,0:T(8,128)(2,1)} %bitcast.62), calls=%async_computation | async-start | bytes 1048576 | tf_op jit(solution)/shard_map/all_to_all | solution.py:49
  88.8 2.1 %copy.36 = bf16[16,32,512]{2,1,0:T(8,128)(2,1)} copy(bf16[16,32,512]{2,0,1:T(8,128)(2,1)} %bitcast.13) | data formatting | bytes 1048576 | tf_op jit(solution)/shard_map/transpose | solution.py:50
  90.9 2.1 %reshape.24 = bf16[16,128,128]{2,1,0:T(8,128)(2,1)} reshape(bf16[16,32,512]{2,1,0:T(8,128)(2,1)} %copy.36) | data formatting | bytes 1048576 | tf_op jit(solution)/shard_map/reshape | solution.py:50
  93.0 2.0 %copy.37 = bf16[16,128,128]{1,2,0:T(8,128)(2,1)} copy(bf16[16,128,128]{2,1,0:T(8,128)(2,1)} %reshape.24) | data formatting | bytes 1048576 | tf_op jit(solution)/shard_map/reshape | solution.py:50
  95.1 3.4 %fusion.38 = f32[256,2048]{0,1} fusion(f32[256,128]{1,0:T(8,128)S(1)} %copy-done.6, bf16[128,2048]{0,1:T(8,128)(2,1)} %bitcast.64), kind=kOutput, calls=%fused_computation.53 | convolution fusion | flops 805306368 | bytes 2752512
  98.5 1.7 %all-to-all-done = bf16[32,16,512]{2,1,0:T(8,128)(2,1)} async-done(((bf16[32,16,512]{2,1,0:T(8,128)(2,1)}), bf16[32,16,512]{2,1,0:T(8,128)(2,1)}, u32[]{:S(2)}, u32[]{:S(2)}) %all-to-all-start) | async-done | bytes 524320 | tf_op jit(solution)/shard_map/all_to_all | solution.py:49
  100.2 2.1 %copy.32 = bf16[16,32,512]{2,1,0:T(8,128)(2,1)} copy(bf16[16,32,512]{2,0,1:T(8,128)(2,1)} %bitcast.7) | data formatting | bytes 1048576 | tf_op jit(solution)/shard_map/transpose | solution.py:50
  102.3 2.2 %reshape.22 = bf16[16,128,128]{2,1,0:T(8,128)(2,1)} reshape(bf16[16,32,512]{2,1,0:T(8,128)(2,1)} %copy.32) | data formatting | bytes 1048576 | tf_op jit(solution)/shard_map/reshape | solution.py:50
  104.5 2.2 %convolution_bitcast_fusion = f32[16,256,128]{1,2,0:T(8,128)S(1)} fusion(bf16[16,128,128]{2,1,0:T(8,128)(2,1)} %reshape.22, f32[256,128,1]{1,0,2:T(8,128)S(1)} %copy-done.2), kind=kOutput, calls=%fused_computation.25 | convolution fusion | flops 805306368 | bytes 2752512 | tf_op jit(solution)/shard_map/kn,cnm->ckm/dot_general | solution.py:26
  107.8 3.5 %fusion.5 = f32[16,128,256]{2,1,0:T(8,128)S(1)} fusion(f32[256,256,1]{1,0,2:T(8,128)S(1)} %copy-done.1, f32[16,128,128]{1,2,0:T(8,128)S(1)} %get-tuple-element.10, f32[16,128,128]{1,2,0:T(8,128)S(1)} %get-tuple-element.9), kind=kOutput, calls=%fused_computation.8 | convolution fusion | flops 1611137024 | bytes 4456448 | tf_op jit(solution)/shard_map/ckm,mf->ckf/dot_general | solution.py:29
  111.3 3.4 %fusion.9 = f32[16,128,256]{2,1,0:T(8,128)S(1)} fusion(f32[256,256,1]{1,0,2:T(8,128)S(1)} %copy-done.1, f32[16,128,128]{1,2,0:T(8,128)S(1)} %get-tuple-element.13, f32[16,128,128]{1,2,0:T(8,128)S(1)} %get-tuple-element.14), kind=kOutput, calls=%fused_computation.12 | convolution fusion | flops 1611137024 | bytes 4456448 | tf_op jit(solution)/shard_map/ckm,mf->ckf/dot_general | solution.py:29
  115.7 2.3 %fusion.13 = f32[16,128,256]{1,2,0:T(8,128)S(1)} fusion(f32[256,256,1]{1,0,2:T(8,128)S(1)} %copy-done.5, f32[16,128,128]{2,1,0:T(8,128)S(1)} %get-tuple-element.6, f32[16,128,128]{2,1,0:T(8,128)S(1)} %get-tuple-element.5), kind=kOutput, calls=%fused_computation.16 | convolution fusion | flops 1611137024 | bytes 4456448 | tf_op jit(solution)/shard_map/ckf,fm->ckm/dot_general | solution.py:35
  118.4 2.6 %fusion.28 = bf16[16,128,128]{1,2,0:T(8,128)(2,1)} fusion(f32[256,128,1]{1,0,2:T(8,128)S(1)} %copy-done.2, f32[16,128,128]{1,2,0:T(8,128)S(1)} %get-tuple-element.8, f32[16,128,128]{1,2,0:T(8,128)S(1)} %get-tuple-element.7), kind=kOutput, calls=%fused_computation.29 | convolution fusion | flops 806092800 | bytes 2752512 | tf_op jit(solution)/shard_map/kn,ckm->cnm/dot_general | solution.py:38
  121.0 2.0 %copy.41 = bf16[16,128,128]{2,1,0:T(8,128)(2,1)} copy(bf16[16,128,128]{1,2,0:T(8,128)(2,1)} %fusion.28) | data formatting | bytes 1048576 | tf_op jit(solution)/shard_map/convert_element_type | solution.py:73
  123.0 2.1 %convert_element_type.52 = bf16[16,32,512]{2,1,0:T(8,128)(2,1)} reshape(bf16[16,128,128]{2,1,0:T(8,128)(2,1)} %copy.41) | data formatting | bytes 1048576 | tf_op jit(solution)/shard_map/convert_element_type | solution.py:73
  126.5 17.0 %all_to_all.15 = bf16[32,16,512]{2,1,0:T(8,128)(2,1)S(1)} all-to-all(bf16[32,16,512]{2,1,0:T(8,128)(2,1)S(1)} %copy.42), channel_id=1, replica_groups=mesh['seq'=32,'chan'=4] {'seq'}, dimensions={0} | all-to-all | bytes 1048576 | tf_op jit(solution)/shard_map/all_to_all | solution.py:74
  144.7 2.5 %copy.43 = f32[512,512]{0,1:T(8,128)} copy(f32[512,512]{1,0:T(8,128)} %bitcast_convert_fusion) | data formatting | bytes 2097152 | tf_op jit(solution)/shard_map/convert_element_type | solution.py:75
  147.2 2.5 %fusion.32 = bf16[512,512]{1,0:T(8,128)(2,1)} fusion(f32[512,3,512]{2,0,1:T(8,128)S(1)} %fusion.24, f32[512,512]{0,1:T(8,128)} %copy.43, f32[512]{0:T(512)S(1)} %copy-done.8), kind=kLoop, calls=%fused_computation.32 | loop fusion | flops 1310720 | bytes 4720640 | tf_op jit(solution)/shard_map/convert_element_type | solution.py:76
  (32 shorter events, 8.5 us)
Async XLA Ops:
  6.5 53.7 %all-gather.2.cloned.1.call-start = ((), (), s32[]{:S(2)}) async-start(), calls=%async_computation.3 | async-start | bytes 5242880 | tf_op jit(solution)/shard_map/all_gather | solution.py:55
  9.5 70.7 %all-to-all-start.1 = ((bf16[32,16,512]{2,1,0:T(8,128)(2,1)}), bf16[32,16,512]{2,1,0:T(8,128)(2,1)}, u32[]{:S(2)}, u32[]{:S(2)}) async-start(bf16[32,16,512]{2,1,0:T(8,128)(2,1)} %bitcast.12), calls=%async_computation.1 | async-start | bytes 1048576 | tf_op jit(solution)/shard_map/all_to_all | solution.py:49
  19.1 55.9 %copy-start.7 = (f32[3,3,512]{2,1,0:T(4,128)S(1)}, f32[3,3,512]{2,1,0:T(4,128)}, u32[]{:S(2)}) copy-start(f32[3,3,512]{2,1,0:T(4,128)} %param.15) | copy-start | bytes 55300
  71.1 4.7 %collective-permute-start = (bf16[2,3,512]{2,0,1:T(2,128)(2,1)S(1)}, bf16[2,3,512]{2,0,1:T(2,128)(2,1)S(1)}, u32[]{:S(2)}, u32[]{:S(2)}) collective-permute-start(bf16[2,3,512]{2,0,1:T(2,128)(2,1)S(1)} %slice.80), channel_id=1, source_target_pairs={{0,4},{4,8},{8,12},{12,16},{16,20},{20,24},{24,28},{28,32},{32,36}... | collective-permute-start | bytes 18440 | tf_op jit(solution)/shard_map/ppermute | solution.py:60
  80.2 14.9 %copy-start.6 = (f32[256,128]{1,0:T(8,128)S(1)}, f32[256,128]{1,0:T(8,128)}, u32[]{:S(2)}) copy-start(f32[256,128]{1,0:T(8,128)} %constant.10.clone) | copy-start | bytes 393220
  80.2 20.0 %all-to-all-start = ((bf16[32,16,512]{2,1,0:T(8,128)(2,1)}), bf16[32,16,512]{2,1,0:T(8,128)(2,1)}, u32[]{:S(2)}, u32[]{:S(2)}) async-start(bf16[32,16,512]{2,1,0:T(8,128)(2,1)} %bitcast.62), calls=%async_computation | async-start | bytes 1048576 | tf_op jit(solution)/shard_map/all_to_all | solution.py:49
  95.1 9.5 %copy-start.2 = (f32[256,128,1]{1,0,2:T(8,128)S(1)}, f32[256,128,1]{1,0,2:T(8,128)}, u32[]{:S(2)}) copy-start(f32[256,128,1]{1,0,2:T(8,128)} %constant.15) | copy-start | bytes 393220
  102.3 4.4 %copy-start.3 = (f32[128,128]{0,1:T(8,128)S(1)}, f32[128,128]{0,1:T(8,128)}, u32[]{:S(2)}) copy-start(f32[128,128]{0,1:T(8,128)} %constant.12.clone) | copy-start | bytes 196612
  102.3 4.4 %copy-start.4 = (f32[128,128]{0,1:T(8,128)S(1)}, f32[128,128]{0,1:T(8,128)}, u32[]{:S(2)}) copy-start(f32[128,128]{0,1:T(8,128)} %constant.11.clone) | copy-start | bytes 196612
  104.5 2.3 %copy-start = (f32[256,2048]{0,1:S(1)}, f32[256,2048]{0,1}, u32[]{:S(2)}) copy-start(f32[256,2048]{0,1} %fusion.38) | copy-start | bytes 6291460
  106.8 1.0 copy-start.1
  114.8 1.0 copy-start.5
  143.5 3.7 %copy-start.8 = (f32[512]{0:T(512)S(1)}, f32[512]{0:T(512)}, u32[]{:S(2)}) copy-start(f32[512]{0:T(512)} %param.17) | copy-start | bytes 6148
Sparse Core Ops, SparseCore 0:
  9.0 51.1 all-gather.1
where the time goes:
time: 158 us; the launch traced here: 157 us
  waiting for transfers between devices  44.3 us (28%)
  matrix products  28.4 us (18%)
  local copies, waits for them, and re-layouts  23.9 us (15%)
  starting transfers between devices  22.1 us (14%)
  blocking collectives  17 us (11%)
  between operations  13.6 us (9%)
  other arithmetic  7.3 us (5%)
    all_gather x1, waiting for transfers between devices, local(): lax.all_gather(tokens, 'chan', axis=1, tiled=True)  41.1 us
    all_to_all x2, starting transfers between devices, to_channels(): parts = lax.all_to_all(parts, 'seq', 0, 0, tiled=True)  18.2 us
    all_to_all x1, blocking collectives, local(): parts = lax.all_to_all(parts, 'seq', 0, 0, tiled=True)  17 us
    dot_general x1, matrix products, local(): jnp.einsum('td,dgc->tgc', lax.all_gather(tokens, 'chan', axis=1, tiled=Tr...  10.9 us
    dot_general x2, matrix products, forward(): b = jnp.einsum('ckm,mf->ckf', turned, mix, precision=exact)  6.98 us
    reshape x3, local copies, waits for them, and re-layouts, to_channels(): return parts.astype(jnp.float32).transpose(1, 0, 2).reshape(own, SIDE, SIDE)  6.37 us
    convert_element_type x3, local copies, waits for them, and re-layouts, local(): result.reshape(own, seq_count, rows).transpose(1, 0, 2).astype(jnp.bfloat16)  5.52 us
    transpose x2, local copies, waits for them, and re-layouts, to_channels(): return parts.astype(jnp.float32).transpose(1, 0, 2).reshape(own, SIDE, SIDE)  4.25 us
  transfers between devices with their start and end apart: 4, of which 3 were waited for; matrix products, arithmetic and copies ran while one was open for 17% of the time, Pallas kernels for 0%

commit v1 on v0

--- a/solution.py
+++ b/solution.py
@@ -52,7 +52,9 @@
     filter_re, filter_im = forward(to_channels(filter_taps), tables)
     projected = jnp.einsum(
         "td,dgc->tgc",
-        lax.all_gather(tokens, "chan", axis=1, tiled=True),
+        jnp.concatenate(
+            lax.all_to_all(jnp.stack([tokens] * lax.axis_size("chan")), "chan", 0, 0), axis=1
+        ),
         in_weight,
         preferred_element_type=jnp.float32,
     ).astype(jnp.bfloat16)

time: 158 us -> 173 us (1.095)
  local copies, waits for them, and re-layouts: 23.9 us -> 41.7 us
  between operations: 13.6 us -> 0.2 us
  waiting for transfers between devices: 44.3 us -> 50.2 us
  starting transfers between devices: 22.1 us -> 27 us
    all_to_all x0 -> x1, waiting for transfers between devices: none -> 47.7 us  [local(): lax.all_to_all(jnp.stack([tokens] * lax.axis_size('chan')), 'chan', 0, 0)]
    all_gather x1 -> x0, waiting for transfers between devices: 41.1 us -> none  [local(): lax.all_gather(tokens, 'chan', axis=1, tiled=True)]
    reshape x0 -> x2, local copies, waits for them, and re-layouts: none -> 15.1 us  [local(): jnp.concatenate(lax.all_to_all(jnp.stack([tokens] * lax.axis_size('chan')...]
    all_to_all x0 -> x1, starting transfers between devices: none -> 4.99 us  [local(): lax.all_to_all(jnp.stack([tokens] * lax.axis_size('chan')), 'chan', 0, 0)]
    another operation x0 -> x1, local copies, waits for them, and re-layouts: none -> 3.75 us  [local(): jnp.stack([tokens] * lax.axis_size('chan'))]
  transfers between devices with their start and end apart: 4 -> 4, of which waited for: 3 -> 3; matrix products, arithmetic and copies ran while one was open for 17% -> 24% of each run, Pallas kernels for 0% -> 0%
where the time goes in v1:
time: 173 us; the launch traced here: 172 us
  waiting for transfers between devices  50.2 us (29%)
  local copies, waits for them, and re-layouts  41.7 us (24%)
  matrix products  28.5 us (16%)
  starting transfers between devices  27 us (16%)
  blocking collectives  17 us (10%)
  other arithmetic  7.28 us (4%)
    all_to_all x1, waiting for transfers between devices, local(): lax.all_to_all(jnp.stack([tokens] * lax.axis_size('chan')), 'chan', 0, 0)  47.7 us
    all_to_all x2, starting transfers between devices, to_channels(): parts = lax.all_to_all(parts, 'seq', 0, 0, tiled=True)  18.4 us
    all_to_all x1, blocking collectives, local(): parts = lax.all_to_all(parts, 'seq', 0, 0, tiled=True)  17 us
    reshape x2, local copies, waits for them, and re-layouts, local(): jnp.concatenate(lax.all_to_all(jnp.stack([tokens] * lax.axis_size('chan')...  15.1 us
    dot_general x1, matrix products, local(): jnp.einsum('td,dgc->tgc', jnp.concatenate(lax.all_to_all(jnp.stack([token...  10.9 us
    dot_general x2, matrix products, forward(): b = jnp.einsum('ckm,mf->ckf', turned, mix, precision=exact)  7.08 us
    reshape x3, local copies, waits for them, and re-layouts, to_channels(): return parts.astype(jnp.float32).transpose(1, 0, 2).reshape(own, SIDE, SIDE)  6.37 us
    convert_element_type x3, local copies, waits for them, and re-layouts, local(): result.reshape(own, seq_count, rows).transpose(1, 0, 2).astype(jnp.bfloat16)  5.52 us
  transfers between devices with their start and end apart: 4, of which 3 were waited for; matrix products, arithmetic and copies ran while one was open for 24% of the time, Pallas kernels for 0%

profile of v1, /device:TPU:1, one launch (start us, length us, event | category | flops | bytes accessed | tf_op | source)
XLA Modules:
  0.0 171.8 jit_solution(3375410867099144503)
XLA Ops:
  0.0 3.7 %stack.2 = bf16[4,512,1024]{2,1,0:T(8,128)(2,1)} broadcast(bf16[512,1024]{1,0:T(8,128)(2,1)} %param.13), dimensions={1,2} | broadcast | bytes 5242880 | tf_op jit(solution)/shard_map/stack | solution.py:56
  3.8 5.0 %all-to-all-start = ((bf16[4,512,1024]{2,1,0:T(8,128)(2,1)}), bf16[4,512,1024]{2,1,0:T(8,128)(2,1)}, u32[]{:S(2)}, u32[]{:S(2)}) async-start(bf16[4,512,1024]{2,1,0:T(8,128)(2,1)} %stack.2), calls=%async_computation | async-start | bytes 8388608 | tf_op jit(solution)/shard_map/all_to_all | solution.py:56
  9.8 47.7 %all-to-all-done = bf16[4,512,1024]{2,1,0:T(8,128)(2,1)} async-done(((bf16[4,512,1024]{2,1,0:T(8,128)(2,1)}), bf16[4,512,1024]{2,1,0:T(8,128)(2,1)}, u32[]{:S(2)}, u32[]{:S(2)}) %all-to-all-start) | async-done | bytes 4194336 | tf_op jit(solution)/shard_map/all_to_all | solution.py:56
  57.5 10.0 %all-to-all-start.2 = ((bf16[32,16,512]{2,1,0:T(8,128)(2,1)}), bf16[32,16,512]{2,1,0:T(8,128)(2,1)}, u32[]{:S(2)}, u32[]{:S(2)}) async-start(bf16[32,16,512]{2,1,0:T(8,128)(2,1)} %bitcast.12), calls=%async_computation.2 | async-start | bytes 1048576 | tf_op jit(solution)/shard_map/all_to_all | solution.py:49
  67.5 7.4 %copy.31 = bf16[512,4,1024]{2,1,0:T(4,128)(2,1)} copy(bf16[512,4,1024]{2,0,1:T(8,128)(2,1)} %bitcast.1) | data formatting | bytes 8388608 | tf_op jit(solution)/shard_map/reshape | solution.py:55
  74.9 7.7 %reshape.36 = bf16[512,4096,1]{1,0,2:T(8,128)(2,1)} reshape(bf16[512,4,1024]{2,1,0:T(4,128)(2,1)} %copy.31) | data formatting | bytes 8388608 | tf_op jit(solution)/shard_map/reshape | solution.py:55
  82.7 10.9 %convolution_convert_fusion = bf16[512,3,512]{2,0,1:T(8,128)(2,1)S(1)} fusion(bf16[512,4096,1]{1,0,2:T(8,128)(2,1)} %reshape.36, bf16[4096,3,512]{2,0,1:T(8,128)(2,1)} %param.14), kind=kOutput, calls=%fused_computation.22 | convolution fusion | flops 6443237376 | bytes 18350080 | tf_op jit(solution)/shard_map/td,dgc->tgc/dot_general | solution.py:53
  93.6 3.5 %collective-permute-start = (bf16[2,3,512]{2,0,1:T(2,128)(2,1)S(1)}, bf16[2,3,512]{2,0,1:T(2,128)(2,1)S(1)}, u32[]{:S(2)}, u32[]{:S(2)}) collective-permute-start(bf16[2,3,512]{2,0,1:T(2,128)(2,1)S(1)} %slice.80), channel_id=1, source_target_pairs={{0,4},{4,8},{8,12},{12,16},{16,20},{20,24},{24,28},{28,32},{32,36}... | collective-permute-start | bytes 18440 | tf_op jit(solution)/shard_map/ppermute | solution.py:62
  100.3 2.0 %copy.32 = bf16[512,512]{1,0:T(8,128)(2,1)} copy(bf16[512,512]{0,1:T(8,128)(2,1)} %convert_bitcast_fusion) | data formatting | bytes 1048576 | tf_op jit(solution)/shard_map/transpose | solution.py:48
  102.3 8.4 %all-to-all-start.1 = ((bf16[32,16,512]{2,1,0:T(8,128)(2,1)}), bf16[32,16,512]{2,1,0:T(8,128)(2,1)}, u32[]{:S(2)}, u32[]{:S(2)}) async-start(bf16[32,16,512]{2,1,0:T(8,128)(2,1)} %bitcast.59), calls=%async_computation.1 | async-start | bytes 1048576 | tf_op jit(solution)/shard_map/all_to_all | solution.py:49
  110.7 2.1 %copy.37 = bf16[16,32,512]{2,1,0:T(8,128)(2,1)} copy(bf16[16,32,512]{2,0,1:T(8,128)(2,1)} %bitcast.13) | data formatting | bytes 1048576 | tf_op jit(solution)/shard_map/transpose | solution.py:50
  112.9 2.1 %reshape.34 = bf16[16,128,128]{2,1,0:T(8,128)(2,1)} reshape(bf16[16,32,512]{2,1,0:T(8,128)(2,1)} %copy.37) | data formatting | bytes 1048576 | tf_op jit(solution)/shard_map/reshape | solution.py:50
  117.1 3.4 %fusion.33 = f32[256,2048]{0,1} fusion(f32[256,128]{1,0:T(8,128)S(1)} %copy-done.7, bf16[128,2048]{0,1:T(8,128)(2,1)} %bitcast.61), kind=kOutput, calls=%fused_computation.51 | convolution fusion | flops 805306368 | bytes 2752512
  122.2 2.1 %copy.33 = bf16[16,32,512]{2,1,0:T(8,128)(2,1)} copy(bf16[16,32,512]{2,0,1:T(8,128)(2,1)} %bitcast.7) | data formatting | bytes 1048576 | tf_op jit(solution)/shard_map/transpose | solution.py:50
  124.3 2.2 %reshape.32 = bf16[16,128,128]{2,1,0:T(8,128)(2,1)} reshape(bf16[16,32,512]{2,1,0:T(8,128)(2,1)} %copy.33) | data formatting | bytes 1048576 | tf_op jit(solution)/shard_map/reshape | solution.py:50
  126.5 2.2 %convolution_bitcast_fusion = f32[16,256,128]{1,2,0:T(8,128)S(1)} fusion(bf16[16,128,128]{2,1,0:T(8,128)(2,1)} %reshape.32, f32[256,128,1]{1,0,2:T(8,128)S(1)} %copy-done.3), kind=kOutput, calls=%fused_computation.23 | convolution fusion | flops 805306368 | bytes 2752512 | tf_op jit(solution)/shard_map/kn,cnm->ckm/dot_general | solution.py:26
  129.7 3.5 %fusion.3 = f32[16,128,256]{2,1,0:T(8,128)S(1)} fusion(f32[256,256,1]{1,0,2:T(8,128)S(1)} %copy-done.1, f32[16,128,128]{1,2,0:T(8,128)S(1)} %get-tuple-element.10, f32[16,128,128]{1,2,0:T(8,128)S(1)} %get-tuple-element.9), kind=kOutput, calls=%fused_computation.6 | convolution fusion | flops 1611137024 | bytes 4456448 | tf_op jit(solution)/shard_map/ckm,mf->ckf/dot_general | solution.py:29
  133.3 3.5 %fusion.7 = f32[16,128,256]{2,1,0:T(8,128)S(1)} fusion(f32[256,256,1]{1,0,2:T(8,128)S(1)} %copy-done.1, f32[16,128,128]{1,2,0:T(8,128)S(1)} %get-tuple-element.13, f32[16,128,128]{1,2,0:T(8,128)S(1)} %get-tuple-element.14), kind=kOutput, calls=%fused_computation.10 | convolution fusion | flops 1611137024 | bytes 4456448 | tf_op jit(solution)/shard_map/ckm,mf->ckf/dot_general | solution.py:29
  137.8 2.3 %fusion.11 = f32[16,128,256]{1,2,0:T(8,128)S(1)} fusion(f32[256,256,1]{1,0,2:T(8,128)S(1)} %copy-done.6, f32[16,128,128]{2,1,0:T(8,128)S(1)} %get-tuple-element.6, f32[16,128,128]{2,1,0:T(8,128)S(1)} %get-tuple-element.5), kind=kOutput, calls=%fused_computation.14 | convolution fusion | flops 1611137024 | bytes 4456448 | tf_op jit(solution)/shard_map/ckf,fm->ckm/dot_general | solution.py:35
  140.4 2.6 %fusion.23 = bf16[16,128,128]{1,2,0:T(8,128)(2,1)} fusion(f32[256,128,1]{1,0,2:T(8,128)S(1)} %copy-done.3, f32[16,128,128]{1,2,0:T(8,128)S(1)} %get-tuple-element.8, f32[16,128,128]{1,2,0:T(8,128)S(1)} %get-tuple-element.7), kind=kOutput, calls=%fused_computation.27 | convolution fusion | flops 806092800 | bytes 2752512 | tf_op jit(solution)/shard_map/kn,ckm->cnm/dot_general | solution.py:38
  145.1 2.1 %convert_element_type.52 = bf16[16,32,512]{2,1,0:T(8,128)(2,1)} reshape(bf16[16,128,128]{2,1,0:T(8,128)(2,1)} %copy.42) | data formatting | bytes 1048576 | tf_op jit(solution)/shard_map/convert_element_type | solution.py:75
  148.6 17.0 %all_to_all.20 = bf16[32,16,512]{2,1,0:T(8,128)(2,1)S(1)} all-to-all(bf16[32,16,512]{2,1,0:T(8,128)(2,1)S(1)} %copy.43), channel_id=1, replica_groups=mesh['seq'=32,'chan'=4] {'seq'}, dimensions={0} | all-to-all | bytes 1048576 | tf_op jit(solution)/shard_map/all_to_all | solution.py:76
  166.8 2.5 %copy.44 = f32[512,512]{0,1:T(8,128)} copy(f32[512,512]{1,0:T(8,128)} %bitcast_convert_fusion) | data formatting | bytes 2097152 | tf_op jit(solution)/shard_map/convert_element_type | solution.py:77
  169.3 2.5 %fusion.27 = bf16[512,512]{1,0:T(8,128)(2,1)} fusion(f32[512,3,512]{2,0,1:T(8,128)S(1)} %fusion.19, f32[512,512]{0,1:T(8,128)} %copy.44, f32[512]{0:T(512)S(1)} %copy-done.9), kind=kLoop, calls=%fused_computation.30 | loop fusion | flops 1310720 | bytes 4720640 | tf_op jit(solution)/shard_map/convert_element_type | solution.py:78
  (36 shorter events, 14.7 us)
Async XLA Ops:
  3.8 5.0 %copy-start.2 = (f32[512,512]{1,0:T(8,128)S(1)}, f32[512,512]{1,0:T(8,128)}, u32[]{:S(2)}) copy-start(f32[512,512]{1,0:T(8,128)} %param.16) | copy-start | bytes 3145732
  3.8 53.8 %all-to-all-start = ((bf16[4,512,1024]{2,1,0:T(8,128)(2,1)}), bf16[4,512,1024]{2,1,0:T(8,128)(2,1)}, u32[]{:S(2)}, u32[]{:S(2)}) async-start(bf16[4,512,1024]{2,1,0:T(8,128)(2,1)} %stack.2), calls=%async_computation | async-start | bytes 8388608 | tf_op jit(solution)/shard_map/all_to_all | solution.py:56
  57.5 44.8 %all-to-all-start.2 = ((bf16[32,16,512]{2,1,0:T(8,128)(2,1)}), bf16[32,16,512]{2,1,0:T(8,128)(2,1)}, u32[]{:S(2)}, u32[]{:S(2)}) async-start(bf16[32,16,512]{2,1,0:T(8,128)(2,1)} %bitcast.12), calls=%async_computation.2 | async-start | bytes 1048576 | tf_op jit(solution)/shard_map/all_to_all | solution.py:49
  82.7 14.5 %copy-start.8 = (f32[3,3,512]{2,1,0:T(4,128)S(1)}, f32[3,3,512]{2,1,0:T(4,128)}, u32[]{:S(2)}) copy-start(f32[3,3,512]{2,1,0:T(4,128)} %param.15) | copy-start | bytes 55300
  93.6 4.3 %collective-permute-start = (bf16[2,3,512]{2,0,1:T(2,128)(2,1)S(1)}, bf16[2,3,512]{2,0,1:T(2,128)(2,1)S(1)}, u32[]{:S(2)}, u32[]{:S(2)}) collective-permute-start(bf16[2,3,512]{2,0,1:T(2,128)(2,1)S(1)} %slice.80), channel_id=1, source_target_pairs={{0,4},{4,8},{8,12},{12,16},{16,20},{20,24},{24,28},{28,32},{32,36}... | collective-permute-start | bytes 18440 | tf_op jit(solution)/shard_map/ppermute | solution.py:62
  102.3 14.7 %copy-start.7 = (f32[256,128]{1,0:T(8,128)S(1)}, f32[256,128]{1,0:T(8,128)}, u32[]{:S(2)}) copy-start(f32[256,128]{1,0:T(8,128)} %constant.10.clone) | copy-start | bytes 393220
  102.3 19.9 %all-to-all-start.1 = ((bf16[32,16,512]{2,1,0:T(8,128)(2,1)}), bf16[32,16,512]{2,1,0:T(8,128)(2,1)}, u32[]{:S(2)}, u32[]{:S(2)}) async-start(bf16[32,16,512]{2,1,0:T(8,128)(2,1)} %bitcast.59), calls=%async_computation.1 | async-start | bytes 1048576 | tf_op jit(solution)/shard_map/all_to_all | solution.py:49
  117.1 9.5 %copy-start.3 = (f32[256,128,1]{1,0,2:T(8,128)S(1)}, f32[256,128,1]{1,0,2:T(8,128)}, u32[]{:S(2)}) copy-start(f32[256,128,1]{1,0,2:T(8,128)} %constant.15) | copy-start | bytes 393220
  124.3 4.4 %copy-start.4 = (f32[128,128]{0,1:T(8,128)S(1)}, f32[128,128]{0,1:T(8,128)}, u32[]{:S(2)}) copy-start(f32[128,128]{0,1:T(8,128)} %constant.12.clone) | copy-start | bytes 196612
  124.3 4.4 %copy-start.5 = (f32[128,128]{0,1:T(8,128)S(1)}, f32[128,128]{0,1:T(8,128)}, u32[]{:S(2)}) copy-start(f32[128,128]{0,1:T(8,128)} %constant.11.clone) | copy-start | bytes 196612
  126.5 2.3 %copy-start = (f32[256,2048]{0,1:S(1)}, f32[256,2048]{0,1}, u32[]{:S(2)}) copy-start(f32[256,2048]{0,1} %fusion.33) | copy-start | bytes 6291460
  128.8 1.0 copy-start.1
  136.8 1.0 copy-start.6
  165.6 3.7 %copy-start.9 = (f32[512]{0:T(512)S(1)}, f32[512]{0:T(512)}, u32[]{:S(2)}) copy-start(f32[512]{0:T(512)} %param.17) | copy-start | bytes 6148
